TPU v7x, 512 devices: a whole 4x4x16 slice. The times are simulated.
512 devices in a mesh: gx: 32 (over y_lo, z), gy: 16 (over x, y_hi, core).
Axes of the slice: x: 4, y: 4 (y_hi: 2, y_lo: 2; y = y_hi * 2 + y_lo), z: 16, core: 2. Of those that a mesh axis runs over, the one named last changes fastest.
Arguments:
- mass_per_volume: float32 [256, 512, 128], P('gx', 'gy'), may hold values from 0.5 to 2
- momentum: float32 [3, 256, 512, 128], P(None, 'gx', 'gy'), may hold values from -0.9 to 0.9
- energy: float32 [256, 512, 128], P('gx', 'gy'), may hold values from 3 to 8
Outputs:
- tendency: float32 [5, 256, 512, 128], P(None, 'gx', 'gy')
- advanced: float32 [5, 256, 512, 128], P(None, 'gx', 'gy')
All inputs are finite; a program needn't handle non-finite values.
Results may differ from a plain program's by a relative error of at most 0.00016.
Values sent between devices are 32-bit elements; how exact they have to be, the bound alone decides.
A program may use at most 64 MiB of HBM per device.

v0:
```python
import jax
import jax.numpy as jnp
import numpy as np
from jax import lax
from jax.sharding import PartitionSpec as P

CX = 8
CY = 8
NZ = 512
HALO = 4
heat_ratio = 1.4
shear_resistance_reference = 0.08
sutherland_power_law = 0.7
prandtl = 0.72
section_step = 0.05
compact_alpha = 1.0 / 3.0
compact_near = 14.0 / 9.0
compact_far = 1.0 / 9.0


def padded(array, sides, width):
    for axis, dim in sides:
        devices, length = (lax.axis_size(axis), array.shape[dim])
        up = [(i, (i + 1) % devices) for i in range(devices)]
        down = [(j, i) for i, j in up]
        last = lax.slice_in_dim(array, length - width, length, axis=dim)
        initial = lax.slice_in_dim(array, 0, width, axis=dim)
        before = lax.ppermute(last, axis, up)
        after = lax.ppermute(initial, axis, down)
        array = jnp.concatenate([before, array, after], axis=dim)
    return array


def tridiagonal_inverse_product(length, stencil):
    solved = np.array(stencil)
    upper_ratio = np.zeros(length)
    for row_index in range(length):
        if row_index == 0:
            pivot_value = 1.0
            solved[row_index] = solved[row_index] / pivot_value
        else:
            pivot_value = 1.0 - compact_alpha * upper_ratio[row_index - 1]
            solved[row_index] = (
                solved[row_index] - compact_alpha * solved[row_index - 1]
            ) / pivot_value
        upper_ratio[row_index] = compact_alpha / pivot_value
    for row_index in range(length - 2, -1, -1):
        solved[row_index] = solved[row_index] - upper_ratio[row_index] * solved[row_index + 1]
    return solved


def compact_matrix(block_size, margin):
    length = block_size + 2 * margin
    stencil = compact_near / 2.0 * (np.eye(length, k=1) - np.eye(length, k=-1))
    stencil = stencil + compact_far / 4.0 * (np.eye(length, k=2) - np.eye(length, k=-2))
    inverse_product = tridiagonal_inverse_product(length, stencil)
    return inverse_product[margin : margin + block_size].astype(np.float32)


def pitch_matrix(total, block_size):
    matrix = compact_matrix(block_size, HALO)
    result = np.zeros((total, total), np.float32)
    rows_all = np.arange(total)
    block_start = rows_all // block_size * block_size
    for offset in range(block_size + 2 * HALO):
        columns = (block_start - HALO + offset) % total
        result[rows_all, columns] += matrix[rows_all % block_size, offset]
    return result


def span_matrix(total):
    offsets = np.arange(total)[:, None] - np.arange(total)[None, :]
    angles = np.pi * offsets / total
    signs = np.where(offsets % 2 == 0, 1.0, -1.0)
    sines = np.where(offsets == 0, 1.0, np.sin(angles))
    result = np.where(offsets == 0, 0.0, np.pi / total * signs * np.cos(angles) / sines)
    return result.astype(np.float32)


def right_side(conserved, gradients_of, derive_x, derive_y, derive_z):
    mass_per_volume = conserved[0]
    momentum = conserved[1:4]
    energy = conserved[4]
    local_speed_vector = momentum / mass_per_volume
    kinetic = 0.5 * jnp.sum(momentum * local_speed_vector, axis=0)
    normal_force_per_area = (heat_ratio - 1.0) * (energy - kinetic)
    thermal_state = normal_force_per_area / mass_per_volume
    basic_quantities = jnp.concatenate([local_speed_vector, thermal_state[None]], 0)
    gradients = gradients_of(basic_quantities)
    shear_resistance = shear_resistance_reference * jnp.power(thermal_state, sutherland_power_law)
    conductivity = shear_resistance * heat_ratio / ((heat_ratio - 1.0) * prandtl)
    dilatation = gradients[0][0] + gradients[1][1] + gradients[2][2]
    derivers = (derive_x, derive_y, derive_z)
    accumulated = None
    for direction in range(3):
        stress_column = [
            shear_resistance * (gradients[direction][component] + gradients[component][direction])
            for component in range(3)
        ]
        stress_column[direction] = (
            stress_column[direction] - 2.0 / 3.0 * shear_resistance * dilatation
        )
        fluxes = [momentum[direction]]
        for component in range(3):
            moment_flux = (
                momentum[component] * local_speed_vector[direction] - stress_column[component]
            )
            if component == direction:
                moment_flux = moment_flux + normal_force_per_area
            fluxes.append(moment_flux)
        work_term = (
            stress_column[0] * local_speed_vector[0]
            + stress_column[1] * local_speed_vector[1]
            + stress_column[2] * local_speed_vector[2]
        )
        fluxes.append(
            (energy + normal_force_per_area) * local_speed_vector[direction]
            - work_term
            - conductivity * gradients[direction][3]
        )
        divergence_part = derivers[direction](jnp.stack(fluxes))
        accumulated = divergence_part if accumulated is None else accumulated + divergence_part
    return -accumulated


def per_device(mass_per_volume, momentum, energy):
    conserved = jnp.concatenate([mass_per_volume[None], momentum, energy[None]], 0)
    highest = lax.Precision.HIGHEST
    x_matrix = jnp.asarray(compact_matrix(CX, HALO))
    z_matrix = jnp.asarray(span_matrix(NZ))

    def apply_x(extended):
        return jnp.einsum("il,flab->fiab", x_matrix, extended, precision=highest)

    def flux_x(values):
        return apply_x(padded(values, (("gx", 1),), HALO))

    y_matrix = jnp.asarray(pitch_matrix(conserved.shape[3], CY))

    def apply_y(values):
        return jnp.einsum("fabk,jk->fabj", values, y_matrix, precision=highest)

    def derive_span(values):
        lines = jnp.transpose(
            lax.all_to_all(values, "gy", split_axis=3, concat_axis=2, tiled=True), (0, 1, 3, 2)
        )
        derived = jnp.einsum("fack,jk->facj", lines, z_matrix, precision=highest)
        returned = lax.all_to_all(derived, "gy", split_axis=3, concat_axis=2, tiled=True)
        return jnp.transpose(returned, (0, 1, 3, 2))

    def gradients_of(basic_quantities):
        extended = padded(basic_quantities, (("gx", 1),), HALO)
        return (apply_x(extended), apply_y(basic_quantities), derive_span(basic_quantities))

    tendency = right_side(conserved, gradients_of, flux_x, apply_y, derive_span)
    advanced = conserved + section_step * tendency
    return (tendency, advanced)


def solution(mesh):
    in_specs = (P("gx", "gy", None), P(None, "gx", "gy", None), P("gx", "gy", None))
    out_specs = (P(None, "gx", "gy", None), P(None, "gx", "gy", None))
    return jax.shard_map(
        per_device, mesh=mesh, in_specs=in_specs, out_specs=out_specs, check_vma=False
    )
```

profile of v0, /device:TPU:7, one launch (start us, length us, event | category | flops | bytes accessed | tf_op | source)
XLA Modules:
  0.0 198.3 jit_solution(11590446967682339407)
XLA Ops:
  5.6 2.9 %copy.103 = f32[4,8,32,128]{2,1,0,3:T(8,128)S(1)} copy(f32[4,8,32,128]{3,1,2,0:T(8,128)} %pad_maximum_fusion) | data formatting | bytes 1048576 | tf_op jit(solution)/shard_map/concatenate | solution.py:88
  10.2 9.6 %all-to-all-start = ((f32[16,1,8192]{2,1,0:T(1,128)}), f32[16,1,8192]{2,1,0:T(1,128)S(1)}, u32[]{:S(2)}, u32[]{:S(2)}) async-start(f32[16,1,8192]{2,1,0:T(1,128)} %reshape.16), calls=%async_computation | async-start | bytes 1048576 | tf_op jit(solution)/shard_map/all_to_all | solution.py:145
  20.6 1.9 collective-permute-start
  22.5 9.4 %collective-permute-start.1 = (f32[4,4,32,128]{3,1,2,0:T(4,128)S(1)}, f32[4,4,32,128]{3,1,2,0:T(4,128)}, u32[]{:S(2)}, u32[]{:S(2)}) collective-permute-start(f32[4,4,32,128]{3,1,2,0:T(4,128)S(1)} %get-tuple-element.27), channel_id=1, source_target_pairs={{16,0},{32,16},{48,32},{64,48},{80,64},{96,80},{112,96},{128,112},... | collective-permute-start | bytes 786440 | tf_op jit(solution)/shard_map/ppermute | solution.py:29
  32.5 2.8 %reduce = f32[16,8192]{1,0:T(8,128)} reduce(f32[16,1,8192]{2,1,0:T(1,128)S(1)} %all-to-all-done, f32[]{:T(128)} %broadcast.6), dimensions={1}, to_apply=%all_to_all.52.reduce_sub_computation | reduce | bytes 1048580 | tf_op jit(solution)/shard_map/all_to_all | solution.py:145
  37.0 2.6 %copy.105 = f32[4,8,16,32,8]{3,2,4,1,0:T(8,128)} copy(f32[4,8,16,32,8]{3,1,0,4,2:T(8,128)S(1)} %bitcast.281) | data formatting | bytes 1048576 | tf_op jit(solution)/shard_map/all_to_all | solution.py:145
  39.6 2.4 %all_to_all.55 = f32[4,8,512,8]{2,3,1,0:T(8,128)S(1)} reshape(f32[4,8,16,32,8]{3,2,4,1,0:T(8,128)} %copy.105) | data formatting | bytes 1048576 | tf_op jit(solution)/shard_map/all_to_all | solution.py:145
  43.0 7.4 %copy.106 = f32[4,8,8,512]{2,1,0,3:T(8,128)} copy(f32[4,8,8,512]{3,2,1,0:T(8,128)S(1)} %fusion.27) | data formatting | bytes 1048576 | tf_op jit(solution)/shard_map/fack,jk->facj/dot_general | solution.py:147
  50.5 7.3 %reshape.18 = f32[16,1,8192]{2,1,0:T(1,128)} reshape(f32[512,4,8,8]{3,2,1,0:T(8,128)} %bitcast.271) | data formatting | bytes 1048576
  57.8 8.2 %all-to-all-start.1 = ((f32[16,1,8192]{2,1,0:T(1,128)}), f32[16,1,8192]{2,1,0:T(1,128)S(1)}, u32[]{:S(2)}, u32[]{:S(2)}) async-start(f32[16,1,8192]{2,1,0:T(1,128)} %reshape.18), calls=%async_computation.1 | async-start | bytes 1048576 | tf_op jit(solution)/shard_map/all_to_all | solution.py:148
  68.1 2.7 %convolution_bitcast_fusion = f32[4,8,32,128]{3,1,2,0:T(8,128)} fusion(f32[8,16,1,1]{1,0,3,2:T(8,128)S(1)} %copy-done.23, f32[4,4,32,128]{3,1,2,0:T(4,128)} %collective-permute-done.1, f32[1,8,32,128]{3,1,2,0:T(8,128)S(1)} %bitcast.275, f32[3,8,32,128]{3,1,2,0:T(8,128)S(1)} %get-tuple-element.28, f32[4,4,32,128]{3,1,2,0:T(4,128)} %collective-permute-done), kind=kOutput, calls=%fused_computation.10 | convolution fusion | flops 25952256 | bytes 1573376 | tf_op jit(solution)/shard_map/il,flab->fiab/dot_general | solution.py:133
  70.8 4.5 %all-to-all-done.1 = f32[16,1,8192]{2,1,0:T(1,128)S(1)} async-done(((f32[16,1,8192]{2,1,0:T(1,128)}), f32[16,1,8192]{2,1,0:T(1,128)S(1)}, u32[]{:S(2)}, u32[]{:S(2)}) %all-to-all-start.1) | async-done | bytes 524320 | tf_op jit(solution)/shard_map/all_to_all | solution.py:148
  77.2 6.7 %reshape.19 = f32[512,4,8,8]{3,2,1,0:T(8,128)} reshape(f32[16,8192]{1,0:T(8,128)S(1)} %reduce.1) | data formatting | bytes 1048576
  83.9 5.2 %copy.107 = f32[4,8,8,16,32]{4,2,3,1,0:T(8,128)S(1)} copy(f32[4,8,8,16,32]{2,1,0,4,3:T(8,128)} %bitcast.270) | data formatting | bytes 1048576 | tf_op jit(solution)/shard_map/all_to_all | solution.py:148
  99.6 2.2 %copy.117 = f32[5,8,32,128]{2,1,0,3:T(8,128)S(1)} copy(f32[5,8,32,128]{3,1,2,0:T(8,128)} %get-tuple-element.20) | data formatting | bytes 1310720 | tf_op jit(solution)/shard_map/stack | solution.py:121
  101.7 2.0 reshape.20
  103.7 6.8 %all-to-all-start.2 = ((f32[16,1,10240]{2,1,0:T(1,128)}), f32[16,1,10240]{2,1,0:T(1,128)S(1)}, u32[]{:S(2)}, u32[]{:S(2)}) async-start(f32[16,1,10240]{2,1,0:T(1,128)} %reshape.20), calls=%async_computation.2 | async-start | bytes 1310720 | tf_op jit(solution)/shard_map/all_to_all | solution.py:145
  113.2 7.9 %all-to-all-done.2 = f32[16,1,10240]{2,1,0:T(1,128)S(1)} async-done(((f32[16,1,10240]{2,1,0:T(1,128)}), f32[16,1,10240]{2,1,0:T(1,128)S(1)}, u32[]{:S(2)}, u32[]{:S(2)}) %all-to-all-start.2) | async-done | bytes 655392 | tf_op jit(solution)/shard_map/all_to_all | solution.py:145
  121.2 3.2 %reduce.2 = f32[16,10240]{1,0:T(8,128)} reduce(f32[16,1,10240]{2,1,0:T(1,128)S(1)} %all-to-all-done.2, f32[]{:T(128)} %broadcast.6), dimensions={1}, to_apply=%all_to_all.60.reduce_sub_computation | reduce | bytes 1310724 | tf_op jit(solution)/shard_map/all_to_all | solution.py:145
  124.3 1.9 reshape.21
  126.3 3.0 %copy.119 = f32[5,8,16,32,8]{3,2,4,1,0:T(8,128)} copy(f32[5,8,16,32,8]{3,1,0,4,2:T(8,128)S(1)} %bitcast.277) | data formatting | bytes 1310720 | tf_op jit(solution)/shard_map/all_to_all | solution.py:145
  129.3 2.6 %all_to_all.63 = f32[5,8,512,8]{2,3,1,0:T(8,128)S(1)} reshape(f32[5,8,16,32,8]{3,2,4,1,0:T(8,128)} %copy.119) | data formatting | bytes 1310720 | tf_op jit(solution)/shard_map/all_to_all | solution.py:145
  133.1 5.5 %copy.120 = f32[5,8,8,512]{2,1,0,3:T(8,128)} copy(f32[5,8,8,512]{3,2,1,0:T(8,128)S(1)} %fusion.25) | data formatting | bytes 1310720 | tf_op jit(solution)/shard_map/fack,jk->facj/dot_general | solution.py:147
  138.6 9.1 %reshape.22 = f32[16,1,10240]{2,1,0:T(1,128)} reshape(f32[512,5,8,8]{3,2,1,0:T(8,128)} %bitcast.268) | data formatting | bytes 1310720
  147.8 6.8 %all-to-all-start.3 = ((f32[16,1,10240]{2,1,0:T(1,128)}), f32[16,1,10240]{2,1,0:T(1,128)S(1)}, u32[]{:S(2)}, u32[]{:S(2)}) async-start(f32[16,1,10240]{2,1,0:T(1,128)} %reshape.22), calls=%async_computation.3 | async-start | bytes 1310720 | tf_op jit(solution)/shard_map/all_to_all | solution.py:148
  154.6 1.9 collective-permute-start.2
  156.5 5.7 %collective-permute-start.3 = (f32[5,4,32,128]{3,1,2,0:T(4,128)}, f32[5,4,32,128]{3,1,2,0:T(4,128)}, u32[]{:S(2)}, u32[]{:S(2)}) collective-permute-start(f32[5,4,32,128]{3,1,2,0:T(4,128)} %get-tuple-element.25), channel_id=1, source_target_pairs={{16,0},{32,16},{48,32},{64,48},{80,64},{96,80},{112,96},{128,112},... | collective-permute-start | bytes 983048 | tf_op jit(solution)/shard_map/ppermute | solution.py:29
  164.0 8.5 %all-to-all-done.3 = f32[16,1,10240]{2,1,0:T(1,128)S(1)} async-done(((f32[16,1,10240]{2,1,0:T(1,128)}), f32[16,1,10240]{2,1,0:T(1,128)S(1)}, u32[]{:S(2)}, u32[]{:S(2)}) %all-to-all-start.3) | async-done | bytes 655392 | tf_op jit(solution)/shard_map/all_to_all | solution.py:148
  172.6 2.2 %reduce.3 = f32[16,10240]{1,0:T(8,128)S(1)} reduce(f32[16,1,10240]{2,1,0:T(1,128)S(1)} %all-to-all-done.3, f32[]{:T(128)} %broadcast.6), dimensions={1}, to_apply=%all_to_all.64.reduce_sub_computation | reduce | bytes 1310724 | tf_op jit(solution)/shard_map/all_to_all | solution.py:148
  174.7 10.4 %reshape.23 = f32[512,5,8,8]{3,2,1,0:T(8,128)} reshape(f32[16,10240]{1,0:T(8,128)S(1)} %reduce.3) | data formatting | bytes 1310720
  185.2 6.6 %copy.121 = f32[5,8,8,16,32]{4,2,3,1,0:T(8,128)S(1)} copy(f32[5,8,8,16,32]{2,1,0,4,3:T(8,128)} %bitcast.269) | data formatting | bytes 1310720 | tf_op jit(solution)/shard_map/all_to_all | solution.py:148
  193.7 2.8 %maximum_add_fusion = (f32[5,8,32,128]{3,1,2,0:T(8,128)S(1)}, f32[5,8,32,128]{3,1,2,0:T(8,128)S(1)}) fusion(f32[1,8,32,128]{3,1,2,0:T(8,128)S(1)} %copy-done.20, f32[3,8,32,128]{3,1,2,0:T(8,128)S(1)} %get-tuple-element.32, f32[1,8,32,128]{3,1,2,0:T(8,128)S(1)} %copy-done.19, f32[5,8,128,32]{2,1,3,0:T(8,128)} %copy.122, f32[5,8,32,128]{3,1,2,0:T(8,128)} %fusion.71, ...), kind=kOutput, calls=%fused_computation.21 | convolution fusion | flops 33259520 | bytes 4588032 | tf_op jit(solution)/shard_map/il,flab->fiab/dot_general | solution.py:133
  (82 shorter events, 34.7 us)
Async XLA Ops:
  4.7 93.1 %copy-start = (f32[8,32,128]{2,0,1:T(8,128)}, f32[8,32,128]{2,0,1:T(8,128)S(1)}, u32[]{:S(2)}) copy-start(f32[8,32,128]{2,0,1:T(8,128)S(1)} %get-tuple-element.19) | copy-start | bytes 393220
  10.2 21.7 %all-to-all-start = ((f32[16,1,8192]{2,1,0:T(1,128)}), f32[16,1,8192]{2,1,0:T(1,128)S(1)}, u32[]{:S(2)}, u32[]{:S(2)}) async-start(f32[16,1,8192]{2,1,0:T(1,128)} %reshape.16), calls=%async_computation | async-start | bytes 1048576 | tf_op jit(solution)/shard_map/all_to_all | solution.py:145
  20.6 47.5 %collective-permute-start = (f32[4,4,32,128]{3,1,2,0:T(4,128)}, f32[4,4,32,128]{3,1,2,0:T(4,128)}, u32[]{:S(2)}, u32[]{:S(2)}) collective-permute-start(f32[4,4,32,128]{3,1,2,0:T(4,128)} %get-tuple-element.26), channel_id=1, source_target_pairs={{0,16},{16,32},{32,48},{48,64},{64,80},{80,96},{96,112},{112,128},... | collective-permute-start | bytes 786440 | tf_op jit(solution)/shard_map/ppermute | solution.py:28
  22.5 45.6 %collective-permute-start.1 = (f32[4,4,32,128]{3,1,2,0:T(4,128)S(1)}, f32[4,4,32,128]{3,1,2,0:T(4,128)}, u32[]{:S(2)}, u32[]{:S(2)}) collective-permute-start(f32[4,4,32,128]{3,1,2,0:T(4,128)S(1)} %get-tuple-element.27), channel_id=1, source_target_pairs={{16,0},{32,16},{48,32},{64,48},{80,64},{96,80},{112,96},{128,112},... | collective-permute-start | bytes 786440 | tf_op jit(solution)/shard_map/ppermute | solution.py:29
  39.6 2.4 %copy-start.2 = (f32[512,512,1,1]{1,0,3,2:T(8,128)S(1)}, f32[512,512,1,1]{1,0,3,2:T(8,128)}, u32[]{:S(2)}) copy-start(f32[512,512,1,1]{1,0,3,2:T(8,128)} %constant.35) | copy-start | bytes 3145732
  50.5 16.2 %copy-start.21 = (f32[128,128,1,1]{1,0,3,2:T(8,128)S(1)}, f32[128,128,1,1]{1,0,3,2:T(8,128)}, u32[]{:S(2)}) copy-start(f32[128,128,1,1]{1,0,3,2:T(8,128)} %constant.34) | copy-start | bytes 196612
  57.8 10.3 %copy-start.23 = (f32[8,16,1,1]{1,0,3,2:T(8,128)S(1)}, f32[8,16,1,1]{1,0,3,2:T(8,128)}, u32[]{:S(2)}) copy-start(f32[8,16,1,1]{1,0,3,2:T(8,128)} %constant.33) | copy-start | bytes 1540
  57.8 17.5 %all-to-all-start.1 = ((f32[16,1,8192]{2,1,0:T(1,128)}), f32[16,1,8192]{2,1,0:T(1,128)S(1)}, u32[]{:S(2)}, u32[]{:S(2)}) async-start(f32[16,1,8192]{2,1,0:T(1,128)} %reshape.18), calls=%async_computation.1 | async-start | bytes 1048576 | tf_op jit(solution)/shard_map/all_to_all | solution.py:148
  90.4 5.4 %copy-start.16 = (f32[4,8,32,128]{3,1,2,0:T(8,128)S(1)}, f32[4,8,32,128]{3,1,2,0:T(8,128)}, u32[]{:S(2)}) copy-start(f32[4,8,32,128]{3,1,2,0:T(8,128)} %convolution_bitcast_fusion) | copy-start | bytes 1572868
  93.9 3.9 %copy-start.10 = (f32[8,32,128]{2,0,1:T(8,128)}, f32[8,32,128]{2,0,1:T(8,128)S(1)}, u32[]{:S(2)}) copy-start(f32[8,32,128]{2,0,1:T(8,128)S(1)} %get-tuple-element.13) | copy-start | bytes 393220
  93.9 3.9 %copy-start.9 = (f32[4,8,128,32]{2,1,3,0:T(8,128)S(1)}, f32[4,8,128,32]{2,1,3,0:T(8,128)}, u32[]{:S(2)}) copy-start(f32[4,8,128,32]{2,1,3,0:T(8,128)} %copy.108) | copy-start | bytes 1572868
  93.9 3.9 %copy-start.14 = (f32[8,32,128]{2,1,0:T(8,128)S(1)}, f32[8,32,128]{2,1,0:T(8,128)}, u32[]{:S(2)}) copy-start(f32[8,32,128]{2,1,0:T(8,128)} %param.8) | copy-start | bytes 393220
  95.8 2.9 %copy-start.4 = (f32[8,32,128]{2,0,1:T(8,128)}, f32[8,32,128]{2,0,1:T(8,128)S(1)}, u32[]{:S(2)}) copy-start(f32[8,32,128]{2,0,1:T(8,128)S(1)} %get-tuple-element.11) | copy-start | bytes 393220
  96.9 1.8 copy-start.12
  97.0 0.8 copy-start.17
  98.7 0.9 copy-start.7
  103.7 8.6 %copy-start.8 = (f32[5,8,32,128]{3,1,2,0:T(8,128)S(1)}, f32[5,8,32,128]{3,1,2,0:T(8,128)}, u32[]{:S(2)}) copy-start(f32[5,8,32,128]{3,1,2,0:T(8,128)} %copy-done.7) | copy-start | bytes 1966084
  103.7 17.4 %all-to-all-start.2 = ((f32[16,1,10240]{2,1,0:T(1,128)}), f32[16,1,10240]{2,1,0:T(1,128)S(1)}, u32[]{:S(2)}, u32[]{:S(2)}) async-start(f32[16,1,10240]{2,1,0:T(1,128)} %reshape.20), calls=%async_computation.2 | async-start | bytes 1310720 | tf_op jit(solution)/shard_map/all_to_all | solution.py:145
  129.3 2.6 %copy-start.3 = (f32[512,512,1,1]{1,0,3,2:T(8,128)S(1)}, f32[512,512,1,1]{1,0,3,2:T(8,128)}, u32[]{:S(2)}) copy-start(f32[512,512,1,1]{1,0,3,2:T(8,128)} %constant.35) | copy-start | bytes 3145732
  138.6 16.0 %copy-start.11 = (f32[8,32,128]{2,0,1:T(8,128)S(1)}, f32[8,32,128]{2,0,1:T(8,128)}, u32[]{:S(2)}) copy-start(f32[8,32,128]{2,0,1:T(8,128)} %copy-done.10) | copy-start | bytes 393220
  138.6 16.0 %copy-start.18 = (f32[5,8,32,128]{3,1,2,0:T(8,128)S(1)}, f32[5,8,32,128]{3,1,2,0:T(8,128)}, u32[]{:S(2)}) copy-start(f32[5,8,32,128]{3,1,2,0:T(8,128)} %bitcast_dynamic-update-slice_fusion.4) | copy-start | bytes 1966084
  138.6 23.7 %copy-start.1 = (f32[8,32,128]{2,0,1:T(8,128)S(1)}, f32[8,32,128]{2,0,1:T(8,128)}, u32[]{:S(2)}) copy-start(f32[8,32,128]{2,0,1:T(8,128)} %copy-done) | copy-start | bytes 393220
  138.6 23.7 %copy-start.5 = (f32[8,32,128]{2,0,1:T(8,128)S(1)}, f32[8,32,128]{2,0,1:T(8,128)}, u32[]{:S(2)}) copy-start(f32[8,32,128]{2,0,1:T(8,128)} %copy-done.4) | copy-start | bytes 393220
  138.6 23.7 %copy-start.6 = (f32[4,8,32,128]{3,1,2,0:T(8,128)S(1)}, f32[4,8,32,128]{3,1,2,0:T(8,128)}, u32[]{:S(2)}) copy-start(f32[4,8,32,128]{3,1,2,0:T(8,128)} %fusion.66) | copy-start | bytes 1572868
  138.6 23.7 %copy-start.13 = (f32[8,32,128]{2,0,1:T(8,128)S(1)}, f32[8,32,128]{2,0,1:T(8,128)}, u32[]{:S(2)}) copy-start(f32[8,32,128]{2,0,1:T(8,128)} %copy-done.12) | copy-start | bytes 393220
  138.6 23.7 %copy-start.15 = (f32[8,32,128]{2,1,0:T(8,128)S(1)}, f32[8,32,128]{2,1,0:T(8,128)}, u32[]{:S(2)}) copy-start(f32[8,32,128]{2,1,0:T(8,128)} %param.8) | copy-start | bytes 393220
  147.8 14.7 %copy-start.22 = (f32[128,128,1,1]{1,0,3,2:T(8,128)S(1)}, f32[128,128,1,1]{1,0,3,2:T(8,128)}, u32[]{:S(2)}) copy-start(f32[128,128,1,1]{1,0,3,2:T(8,128)} %constant.34) | copy-start | bytes 196612
  147.8 24.8 %all-to-all-start.3 = ((f32[16,1,10240]{2,1,0:T(1,128)}), f32[16,1,10240]{2,1,0:T(1,128)S(1)}, u32[]{:S(2)}, u32[]{:S(2)}) async-start(f32[16,1,10240]{2,1,0:T(1,128)} %reshape.22), calls=%async_computation.3 | async-start | bytes 1310720 | tf_op jit(solution)/shard_map/all_to_all | solution.py:148
  154.6 39.0 %collective-permute-start.2 = (f32[5,4,32,128]{3,1,2,0:T(4,128)}, f32[5,4,32,128]{3,1,2,0:T(4,128)}, u32[]{:S(2)}, u32[]{:S(2)}) collective-permute-start(f32[5,4,32,128]{3,1,2,0:T(4,128)} %get-tuple-element.24), channel_id=1, source_target_pairs={{0,16},{16,32},{32,48},{48,64},{64,80},{80,96},{96,112},{112,128},... | collective-permute-start | bytes 983048 | tf_op jit(solution)/shard_map/ppermute | solution.py:28
  156.5 37.1 %collective-permute-start.3 = (f32[5,4,32,128]{3,1,2,0:T(4,128)}, f32[5,4,32,128]{3,1,2,0:T(4,128)}, u32[]{:S(2)}, u32[]{:S(2)}) collective-permute-start(f32[5,4,32,128]{3,1,2,0:T(4,128)} %get-tuple-element.25), channel_id=1, source_target_pairs={{16,0},{32,16},{48,32},{64,48},{80,64},{96,80},{112,96},{128,112},... | collective-permute-start | bytes 983048 | tf_op jit(solution)/shard_map/ppermute | solution.py:29
  191.8 1.9 copy-start.19
  191.8 1.8 copy-start.20
where the time goes:
time: 200 us; the launch traced here: 198 us
  local copies, waits for them, and re-layouts  91.3 us (46%)
  starting transfers between devices  50.4 us (25%)
  other arithmetic  24.1 us (12%)
  waiting for transfers between devices  20.9 us (10%)
  matrix products  10.7 us (5%)
    unnamed x60, local copies, waits for them, and re-layouts  46.2 us
    all_to_all x2, starting transfers between devices, derive_span(): lax.all_to_all(values, 'gy', split_axis=3, concat_axis=2, tiled=True)  16.4 us
    ppermute x2, starting transfers between devices, padded(): after = lax.ppermute(initial, axis, down)  15.1 us
    all_to_all x2, starting transfers between devices, derive_span(): lax.all_to_all(derived, 'gy', split_axis=3, concat_axis=2, tiled=True)  15 us
    all_to_all x4, local copies, waits for them, and re-layouts, derive_span(): lax.all_to_all(derived, 'gy', split_axis=3, concat_axis=2, tiled=True)  15 us
    all_to_all x2, waiting for transfers between devices, derive_span(): lax.all_to_all(derived, 'gy', split_axis=3, concat_axis=2, tiled=True)  13 us
    dot_general x2, local copies, waits for them, and re-layouts, derive_span(): derived = jnp.einsum('fack,jk->facj', lines, z_matrix, precision=highest)  12.9 us
    all_to_all x5, local copies, waits for them, and re-layouts, derive_span(): lax.all_to_all(values, 'gy', split_axis=3, concat_axis=2, tiled=True)  11.1 us
  transfers between devices with their start and end apart: 8, of which 3 were waited for; matrix products, arithmetic and copies ran while one was open for 27% of the time, Pallas kernels for 0%

commit v1 on v0

--- a/solution.py
+++ b/solution.py
@@ -145,7 +145,10 @@
             lax.all_to_all(values, "gy", split_axis=3, concat_axis=2, tiled=True), (0, 1, 3, 2)
         )
         derived = jnp.einsum("fack,jk->facj", lines, z_matrix, precision=highest)
-        returned = lax.all_to_all(derived, "gy", split_axis=3, concat_axis=2, tiled=True)
+        returned = jnp.concatenate(
+            lax.all_to_all(jnp.stack(jnp.split(derived, lax.axis_size("gy"), axis=3)), "gy", 0, 0),
+            axis=2,
+        )
         return jnp.transpose(returned, (0, 1, 3, 2))
 
     def gradients_of(basic_quantities):

time: 200 us -> 168 us (0.84)
  local copies, waits for them, and re-layouts: 91.3 us -> 60.3 us
    all_to_all x4 -> x0, local copies, waits for them, and re-layouts: 15 us -> none  [derive_span(): lax.all_to_all(derived, 'gy', split_axis=3, concat_axis=2, tiled=True)]
    dot_general x2 -> x0, local copies, waits for them, and re-layouts: 12.9 us -> none  [derive_span(): derived = jnp.einsum('fack,jk->facj', lines, z_matrix, precision=highest)]
    unnamed x60 -> x94, local copies, waits for them, and re-layouts: 46.2 us -> 33.9 us
    reshape x0 -> x4, local copies, waits for them, and re-layouts: none -> 8.38 us  [derive_span(): jnp.concatenate(lax.all_to_all(jnp.stack(jnp.split(derived, lax.axis_size...]
    unnamed x8, other arithmetic: 8.32 us -> 6.26 us
  transfers between devices with their start and end apart: 8 -> 8, of which waited for: 3 -> 3; matrix products, arithmetic and copies ran while one was open for 27% -> 19% of each run, Pallas kernels for 0% -> 0%
where the time goes in v1:
time: 168 us; the launch traced here: 167 us
  local copies, waits for them, and re-layouts  60.3 us (36%)
  starting transfers between devices  50.2 us (30%)
  other arithmetic  24 us (14%)
  waiting for transfers between devices  21 us (12%)
  matrix products  10 us (6%)
    unnamed x94, local copies, waits for them, and re-layouts  33.9 us
    all_to_all x2, starting transfers between devices, derive_span(): lax.all_to_all(values, 'gy', split_axis=3, concat_axis=2, tiled=True)  16.4 us
    ppermute x2, starting transfers between devices, padded(): after = lax.ppermute(initial, axis, down)  15.1 us
    all_to_all x2, starting transfers between devices, derive_span(): lax.all_to_all(jnp.stack(jnp.split(derived, lax.axis_size('gy'), axis=3))...  14.9 us
    all_to_all x2, waiting for transfers between devices, derive_span(): lax.all_to_all(jnp.stack(jnp.split(derived, lax.axis_size('gy'), axis=3))...  13.1 us
    all_to_all x5, local copies, waits for them, and re-layouts, derive_span(): lax.all_to_all(values, 'gy', split_axis=3, concat_axis=2, tiled=True)  11.1 us
    reshape x4, local copies, waits for them, and re-layouts, derive_span(): jnp.concatenate(lax.all_to_all(jnp.stack(jnp.split(derived, lax.axis_size...  8.38 us
    all_to_all x2, waiting for transfers between devices, derive_span(): lax.all_to_all(values, 'gy', split_axis=3, concat_axis=2, tiled=True)  7.93 us
  transfers between devices with their start and end apart: 8, of which 3 were waited for; matrix products, arithmetic and copies ran while one was open for 19% of the time, Pallas kernels for 0%

profile of v1, /device:TPU:7, one launch (start us, length us, event | category | flops | bytes accessed | tf_op | source)
XLA Modules:
  0.0 166.6 jit_solution(9277754265185258246)
XLA Ops:
  2.9 1.9 %copy_divide_fusion = (f32[8,32,128]{2,0,1:T(8,128)S(1)}, f32[8,32,128]{2,0,1:T(8,128)S(1)}, f32[1,8,32,128]{3,1,2,0:T(8,128)}, f32[1,8,32,128]{3,1,2,0:T(8,128)}) fusion(f32[8,32,128]{2,1,0:T(8,128)} %param.6, f32[8,32,128]{2,0,1:T(8,128)S(1)} %get-tuple-element.29, f32[8,32,128]{2,1,0:T(8,128)} %param.8), kind=kLoop, calls=%fused_computation.172 | loop fusion | flops 131072 | bytes 917504 | tf_op jit(solution)/shard_map/div | solution.py:87
  5.6 2.9 %copy.101 = f32[4,8,32,128]{2,1,0,3:T(8,128)S(1)} copy(f32[4,8,32,128]{3,1,2,0:T(8,128)} %pad_maximum_fusion) | data formatting | bytes 1048576 | tf_op jit(solution)/shard_map/concatenate | solution.py:88
  10.2 9.6 %all-to-all-start = ((f32[16,1,8192]{2,1,0:T(1,128)}), f32[16,1,8192]{2,1,0:T(1,128)S(1)}, u32[]{:S(2)}, u32[]{:S(2)}) async-start(f32[16,1,8192]{2,1,0:T(1,128)} %reshape.32), calls=%async_computation | async-start | bytes 1048576 | tf_op jit(solution)/shard_map/all_to_all | solution.py:145
  20.6 1.9 %collective-permute-start = (f32[4,4,32,128]{3,1,2,0:T(4,128)}, f32[4,4,32,128]{3,1,2,0:T(4,128)}, u32[]{:S(2)}, u32[]{:S(2)}) collective-permute-start(f32[4,4,32,128]{3,1,2,0:T(4,128)} %get-tuple-element.26), channel_id=1, source_target_pairs={{0,16},{16,32},{32,48},{48,64},{64,80},{80,96},{96,112},{112,128},... | collective-permute-start | bytes 786440 | tf_op jit(solution)/shard_map/ppermute | solution.py:28
  22.5 9.4 %collective-permute-start.1 = (f32[4,4,32,128]{3,1,2,0:T(4,128)S(1)}, f32[4,4,32,128]{3,1,2,0:T(4,128)}, u32[]{:S(2)}, u32[]{:S(2)}) collective-permute-start(f32[4,4,32,128]{3,1,2,0:T(4,128)S(1)} %get-tuple-element.27), channel_id=1, source_target_pairs={{16,0},{32,16},{48,32},{64,48},{80,64},{96,80},{112,96},{128,112},... | collective-permute-start | bytes 786440 | tf_op jit(solution)/shard_map/ppermute | solution.py:29
  32.5 2.8 %reduce = f32[16,8192]{1,0:T(8,128)} reduce(f32[16,1,8192]{2,1,0:T(1,128)S(1)} %all-to-all-done, f32[]{:T(128)} %broadcast.6), dimensions={1}, to_apply=%all_to_all.32.reduce_sub_computation | reduce | bytes 1048580 | tf_op jit(solution)/shard_map/all_to_all | solution.py:145
  37.0 2.6 %copy.103 = f32[4,8,16,32,8]{3,2,4,1,0:T(8,128)} copy(f32[4,8,16,32,8]{3,1,0,4,2:T(8,128)S(1)} %bitcast.401) | data formatting | bytes 1048576 | tf_op jit(solution)/shard_map/all_to_all | solution.py:145
  39.5 2.4 %all_to_all.35 = f32[4,8,512,8]{2,3,1,0:T(8,128)S(1)} reshape(f32[4,8,16,32,8]{3,2,4,1,0:T(8,128)} %copy.103) | data formatting | bytes 1048576 | tf_op jit(solution)/shard_map/all_to_all | solution.py:145
  46.1 8.1 %all-to-all-start.1 = ((f32[16,1,8192]{2,1,0:T(1,128)}), f32[16,1,8192]{2,1,0:T(1,128)S(1)}, u32[]{:S(2)}, u32[]{:S(2)}) async-start(f32[16,1,8192]{2,1,0:T(1,128)} %reshape.34), calls=%async_computation.1 | async-start | bytes 1048576 | tf_op jit(solution)/shard_map/all_to_all | solution.py:149
  56.2 2.7 %convolution_bitcast_fusion = f32[4,8,32,128]{3,1,2,0:T(8,128)} fusion(f32[8,16,1,1]{1,0,3,2:T(8,128)S(1)} %copy-done.25, f32[4,4,32,128]{3,1,2,0:T(4,128)} %collective-permute-done.1, f32[1,8,32,128]{3,1,2,0:T(8,128)S(1)} %bitcast.397, f32[3,8,32,128]{3,1,2,0:T(8,128)S(1)} %get-tuple-element.28, f32[4,4,32,128]{3,1,2,0:T(4,128)} %collective-permute-done), kind=kOutput, calls=%fused_computation.12 | convolution fusion | flops 25952256 | bytes 1573376 | tf_op jit(solution)/shard_map/il,flab->fiab/dot_general | solution.py:133
  58.9 4.6 %all-to-all-done.1 = f32[16,1,8192]{2,1,0:T(1,128)S(1)} async-done(((f32[16,1,8192]{2,1,0:T(1,128)}), f32[16,1,8192]{2,1,0:T(1,128)S(1)}, u32[]{:S(2)}, u32[]{:S(2)}) %all-to-all-start.1) | async-done | bytes 524320 | tf_op jit(solution)/shard_map/all_to_all | solution.py:149
  63.5 2.8 %reduce.1 = f32[16,8192]{1,0:T(8,128)} reduce(f32[16,1,8192]{2,1,0:T(1,128)S(1)} %all-to-all-done.1, f32[]{:T(128)} %broadcast.6), dimensions={1}, to_apply=%all_to_all.36.reduce_sub_computation | reduce | bytes 1048580 | tf_op jit(solution)/shard_map/all_to_all | solution.py:149
  69.6 2.2 %copy.105 = f32[4,8,128,32]{2,1,3,0:T(8,128)S(1)} copy(f32[4,8,128,32]{3,2,1,0:T(8,128)} %copy_bitcast_fusion.1) | data formatting | bytes 1048576 | tf_op jit(solution)/shard_map/reshape | solution.py:148
  78.9 2.2 %copy.114 = f32[5,8,32,128]{2,1,0,3:T(8,128)S(1)} copy(f32[5,8,32,128]{3,1,2,0:T(8,128)} %get-tuple-element.20) | data formatting | bytes 1310720 | tf_op jit(solution)/shard_map/stack | solution.py:121
  81.1 2.0 %reshape.36 = f32[16,1,10240]{2,1,0:T(1,128)} reshape(f32[128,5,8,32]{3,2,1,0:T(8,128)S(1)} %bitcast.398) | data formatting | bytes 1310720
  83.0 6.8 %all-to-all-start.2 = ((f32[16,1,10240]{2,1,0:T(1,128)}), f32[16,1,10240]{2,1,0:T(1,128)S(1)}, u32[]{:S(2)}, u32[]{:S(2)}) async-start(f32[16,1,10240]{2,1,0:T(1,128)} %reshape.36), calls=%async_computation.2 | async-start | bytes 1310720 | tf_op jit(solution)/shard_map/all_to_all | solution.py:145
  89.8 1.8 %bitcast_dynamic-update-slice_fusion.4 = f32[5,8,32,128]{3,1,2,0:T(8,128)} fusion(f32[5,8,32,128]{3,1,2,0:T(8,128)} %copy-done.19, f32[8,32,128]{2,0,1:T(8,128)} %copy-done, f32[3,8,32,128]{3,1,2,0:T(8,128)S(1)} %get-tuple-element.32, f32[3,8,32,128]{3,1,2,0:T(8,128)S(1)} %get-tuple-element.28, f32[8,32,128]{2,0,1:T(8,128)} %copy-done.4, ...), kind=kLoop, calls=%fused_computation.131 | loop fusion | flops 229376 | bytes 917504
  92.6 7.9 %all-to-all-done.2 = f32[16,1,10240]{2,1,0:T(1,128)S(1)} async-done(((f32[16,1,10240]{2,1,0:T(1,128)}), f32[16,1,10240]{2,1,0:T(1,128)S(1)}, u32[]{:S(2)}, u32[]{:S(2)}) %all-to-all-start.2) | async-done | bytes 655392 | tf_op jit(solution)/shard_map/all_to_all | solution.py:145
  100.5 3.2 %reduce.2 = f32[16,10240]{1,0:T(8,128)} reduce(f32[16,1,10240]{2,1,0:T(1,128)S(1)} %all-to-all-done.2, f32[]{:T(128)} %broadcast.6), dimensions={1}, to_apply=%all_to_all.37.reduce_sub_computation | reduce | bytes 1310724 | tf_op jit(solution)/shard_map/all_to_all | solution.py:145
  103.7 1.9 %reshape.37 = f32[128,5,8,32]{3,2,1,0:T(8,128)S(1)} reshape(f32[16,10240]{1,0:T(8,128)} %reduce.2) | data formatting | bytes 1310720
  105.6 3.0 %copy.116 = f32[5,8,16,32,8]{3,2,4,1,0:T(8,128)} copy(f32[5,8,16,32,8]{3,1,0,4,2:T(8,128)S(1)} %bitcast.399) | data formatting | bytes 1310720 | tf_op jit(solution)/shard_map/all_to_all | solution.py:145
  108.6 2.6 %all_to_all.40 = f32[5,8,512,8]{2,3,1,0:T(8,128)S(1)} reshape(f32[5,8,16,32,8]{3,2,4,1,0:T(8,128)} %copy.116) | data formatting | bytes 1310720 | tf_op jit(solution)/shard_map/all_to_all | solution.py:145
  124.6 3.5 %reshape.38 = f32[16,1,10240]{2,1,0:T(1,128)} reshape(f32[16,5,8,8,32]{4,3,2,1,0:T(8,128)} %fusion.31) | data formatting | bytes 1310720
  128.1 6.8 %all-to-all-start.3 = ((f32[16,1,10240]{2,1,0:T(1,128)}), f32[16,1,10240]{2,1,0:T(1,128)S(1)}, u32[]{:S(2)}, u32[]{:S(2)}) async-start(f32[16,1,10240]{2,1,0:T(1,128)} %reshape.38), calls=%async_computation.3 | async-start | bytes 1310720 | tf_op jit(solution)/shard_map/all_to_all | solution.py:149
  134.9 1.9 %collective-permute-start.2 = (f32[5,4,32,128]{3,1,2,0:T(4,128)}, f32[5,4,32,128]{3,1,2,0:T(4,128)}, u32[]{:S(2)}, u32[]{:S(2)}) collective-permute-start(f32[5,4,32,128]{3,1,2,0:T(4,128)} %get-tuple-element.24), channel_id=1, source_target_pairs={{0,16},{16,32},{32,48},{48,64},{64,80},{80,96},{96,112},{112,128},... | collective-permute-start | bytes 983048 | tf_op jit(solution)/shard_map/ppermute | solution.py:28
  136.8 5.7 %collective-permute-start.3 = (f32[5,4,32,128]{3,1,2,0:T(4,128)}, f32[5,4,32,128]{3,1,2,0:T(4,128)}, u32[]{:S(2)}, u32[]{:S(2)}) collective-permute-start(f32[5,4,32,128]{3,1,2,0:T(4,128)} %get-tuple-element.25), channel_id=1, source_target_pairs={{16,0},{32,16},{48,32},{64,48},{80,64},{96,80},{112,96},{128,112},... | collective-permute-start | bytes 983048 | tf_op jit(solution)/shard_map/ppermute | solution.py:29
  144.3 8.5 %all-to-all-done.3 = f32[16,1,10240]{2,1,0:T(1,128)S(1)} async-done(((f32[16,1,10240]{2,1,0:T(1,128)}), f32[16,1,10240]{2,1,0:T(1,128)S(1)}, u32[]{:S(2)}, u32[]{:S(2)}) %all-to-all-start.3) | async-done | bytes 655392 | tf_op jit(solution)/shard_map/all_to_all | solution.py:149
  152.9 3.2 %reduce.3 = f32[16,10240]{1,0:T(8,128)} reduce(f32[16,1,10240]{2,1,0:T(1,128)S(1)} %all-to-all-done.3, f32[]{:T(128)} %broadcast.6), dimensions={1}, to_apply=%all_to_all.41.reduce_sub_computation | reduce | bytes 1310724 | tf_op jit(solution)/shard_map/all_to_all | solution.py:149
  156.0 1.9 %reshape.39 = f32[16,5,8,8,32]{4,3,2,1,0:T(8,128)S(1)} reshape(f32[16,10240]{1,0:T(8,128)} %reduce.3) | data formatting | bytes 1310720
  158.0 1.8 %copy_bitcast_fusion = f32[5,8,128,32]{3,2,1,0:T(8,128)} fusion(f32[16,5,8,8,32]{4,3,2,1,0:T(8,128)S(1)} %reshape.39), kind=kLoop, calls=%fused_computation | loop fusion | bytes 1310720 | tf_op jit(solution)/shard_map/reshape | solution.py:148
  159.8 2.7 %copy.118 = f32[5,8,128,32]{2,1,3,0:T(8,128)S(1)} copy(f32[5,8,128,32]{3,2,1,0:T(8,128)} %copy_bitcast_fusion) | data formatting | bytes 1310720 | tf_op jit(solution)/shard_map/reshape | solution.py:148
  162.6 2.2 %maximum_add_fusion = (f32[5,8,32,128]{3,1,2,0:T(8,128)S(1)}, f32[5,8,32,128]{3,1,2,0:T(8,128)S(1)}) fusion(f32[1,8,32,128]{3,1,2,0:T(8,128)S(1)} %copy-done.22, f32[3,8,32,128]{3,1,2,0:T(8,128)S(1)} %get-tuple-element.32, f32[1,8,32,128]{3,1,2,0:T(8,128)S(1)} %copy-done.21, f32[5,8,128,32]{2,1,3,0:T(8,128)S(1)} %copy.118, ...), kind=kOutput, calls=%fused_computation.23 | convolution fusion | flops 33259520 | bytes 4588032 | tf_op jit(solution)/shard_map/il,flab->fiab/dot_general | solution.py:133
  (116 shorter events, 42.2 us)
Async XLA Ops:
  4.8 72.4 %copy-start = (f32[8,32,128]{2,0,1:T(8,128)}, f32[8,32,128]{2,0,1:T(8,128)S(1)}, u32[]{:S(2)}) copy-start(f32[8,32,128]{2,0,1:T(8,128)S(1)} %get-tuple-element.19) | copy-start | bytes 393220
  10.2 21.7 %all-to-all-start = ((f32[16,1,8192]{2,1,0:T(1,128)}), f32[16,1,8192]{2,1,0:T(1,128)S(1)}, u32[]{:S(2)}, u32[]{:S(2)}) async-start(f32[16,1,8192]{2,1,0:T(1,128)} %reshape.32), calls=%async_computation | async-start | bytes 1048576 | tf_op jit(solution)/shard_map/all_to_all | solution.py:145
  20.6 35.6 %collective-permute-start = (f32[4,4,32,128]{3,1,2,0:T(4,128)}, f32[4,4,32,128]{3,1,2,0:T(4,128)}, u32[]{:S(2)}, u32[]{:S(2)}) collective-permute-start(f32[4,4,32,128]{3,1,2,0:T(4,128)} %get-tuple-element.26), channel_id=1, source_target_pairs={{0,16},{16,32},{32,48},{48,64},{64,80},{80,96},{96,112},{112,128},... | collective-permute-start | bytes 786440 | tf_op jit(solution)/shard_map/ppermute | solution.py:28
  22.5 33.7 %collective-permute-start.1 = (f32[4,4,32,128]{3,1,2,0:T(4,128)S(1)}, f32[4,4,32,128]{3,1,2,0:T(4,128)}, u32[]{:S(2)}, u32[]{:S(2)}) collective-permute-start(f32[4,4,32,128]{3,1,2,0:T(4,128)S(1)} %get-tuple-element.27), channel_id=1, source_target_pairs={{16,0},{32,16},{48,32},{64,48},{80,64},{96,80},{112,96},{128,112},... | collective-permute-start | bytes 786440 | tf_op jit(solution)/shard_map/ppermute | solution.py:29
  39.5 2.4 %copy-start.2 = (f32[512,512,1,1]{1,0,3,2:T(8,128)S(1)}, f32[512,512,1,1]{1,0,3,2:T(8,128)}, u32[]{:S(2)}) copy-start(f32[512,512,1,1]{1,0,3,2:T(8,128)} %constant.35) | copy-start | bytes 3145732
  44.2 10.6 %copy-start.23 = (f32[128,128,1,1]{1,0,3,2:T(8,128)S(1)}, f32[128,128,1,1]{1,0,3,2:T(8,128)}, u32[]{:S(2)}) copy-start(f32[128,128,1,1]{1,0,3,2:T(8,128)} %constant.34) | copy-start | bytes 196612
  44.3 11.9 %copy-start.25 = (f32[8,16,1,1]{1,0,3,2:T(8,128)S(1)}, f32[8,16,1,1]{1,0,3,2:T(8,128)}, u32[]{:S(2)}) copy-start(f32[8,16,1,1]{1,0,3,2:T(8,128)} %constant.33) | copy-start | bytes 1540
  46.1 17.4 %all-to-all-start.1 = ((f32[16,1,8192]{2,1,0:T(1,128)}), f32[16,1,8192]{2,1,0:T(1,128)S(1)}, u32[]{:S(2)}, u32[]{:S(2)}) async-start(f32[16,1,8192]{2,1,0:T(1,128)} %reshape.34), calls=%async_computation.1 | async-start | bytes 1048576 | tf_op jit(solution)/shard_map/all_to_all | solution.py:149
  69.6 4.0 %copy-start.6 = (f32[4,8,32,128]{3,1,2,0:T(8,128)S(1)}, f32[4,8,32,128]{3,1,2,0:T(8,128)}, u32[]{:S(2)}) copy-start(f32[4,8,32,128]{3,1,2,0:T(8,128)} %fusion.98) | copy-start | bytes 1572868
  71.8 4.2 %copy-start.18 = (f32[4,8,32,128]{3,1,2,0:T(8,128)S(1)}, f32[4,8,32,128]{3,1,2,0:T(8,128)}, u32[]{:S(2)}) copy-start(f32[4,8,32,128]{3,1,2,0:T(8,128)} %convolution_bitcast_fusion) | copy-start | bytes 1572868
  74.3 2.9 %copy-start.12 = (f32[8,32,128]{2,0,1:T(8,128)}, f32[8,32,128]{2,0,1:T(8,128)S(1)}, u32[]{:S(2)}) copy-start(f32[8,32,128]{2,0,1:T(8,128)S(1)} %get-tuple-element.13) | copy-start | bytes 393220
  74.3 2.9 %copy-start.16 = (f32[8,32,128]{2,1,0:T(8,128)S(1)}, f32[8,32,128]{2,1,0:T(8,128)}, u32[]{:S(2)}) copy-start(f32[8,32,128]{2,1,0:T(8,128)} %param.8) | copy-start | bytes 393220
  76.1 2.0 %copy-start.4 = (f32[8,32,128]{2,0,1:T(8,128)}, f32[8,32,128]{2,0,1:T(8,128)S(1)}, u32[]{:S(2)}) copy-start(f32[8,32,128]{2,0,1:T(8,128)S(1)} %get-tuple-element.11) | copy-start | bytes 393220
  76.3 1.8 %copy-start.14 = (f32[8,32,128]{2,0,1:T(8,128)}, f32[8,32,128]{2,0,1:T(8,128)S(1)}, u32[]{:S(2)}) copy-start(f32[8,32,128]{2,0,1:T(8,128)S(1)} %get-tuple-element.17) | copy-start | bytes 393220
  83.0 8.6 %copy-start.9 = (f32[5,8,32,128]{3,1,2,0:T(8,128)S(1)}, f32[5,8,32,128]{3,1,2,0:T(8,128)}, u32[]{:S(2)}) copy-start(f32[5,8,32,128]{3,1,2,0:T(8,128)} %copy-done.8) | copy-start | bytes 1966084
  83.0 17.4 %all-to-all-start.2 = ((f32[16,1,10240]{2,1,0:T(1,128)}), f32[16,1,10240]{2,1,0:T(1,128)S(1)}, u32[]{:S(2)}, u32[]{:S(2)}) async-start(f32[16,1,10240]{2,1,0:T(1,128)} %reshape.36), calls=%async_computation.2 | async-start | bytes 1310720 | tf_op jit(solution)/shard_map/all_to_all | solution.py:145
  108.6 2.6 %copy-start.3 = (f32[512,512,1,1]{1,0,3,2:T(8,128)S(1)}, f32[512,512,1,1]{1,0,3,2:T(8,128)}, u32[]{:S(2)}) copy-start(f32[512,512,1,1]{1,0,3,2:T(8,128)} %constant.35) | copy-start | bytes 3145732
  124.5 10.3 %copy-start.13 = (f32[8,32,128]{2,0,1:T(8,128)S(1)}, f32[8,32,128]{2,0,1:T(8,128)}, u32[]{:S(2)}) copy-start(f32[8,32,128]{2,0,1:T(8,128)} %copy-done.12) | copy-start | bytes 393220
  124.5 10.3 %copy-start.20 = (f32[5,8,32,128]{3,1,2,0:T(8,128)S(1)}, f32[5,8,32,128]{3,1,2,0:T(8,128)}, u32[]{:S(2)}) copy-start(f32[5,8,32,128]{3,1,2,0:T(8,128)} %bitcast_dynamic-update-slice_fusion.4) | copy-start | bytes 1966084
  124.5 18.0 %copy-start.1 = (f32[8,32,128]{2,0,1:T(8,128)S(1)}, f32[8,32,128]{2,0,1:T(8,128)}, u32[]{:S(2)}) copy-start(f32[8,32,128]{2,0,1:T(8,128)} %copy-done) | copy-start | bytes 393220
  124.6 18.0 %copy-start.5 = (f32[8,32,128]{2,0,1:T(8,128)S(1)}, f32[8,32,128]{2,0,1:T(8,128)}, u32[]{:S(2)}) copy-start(f32[8,32,128]{2,0,1:T(8,128)} %copy-done.4) | copy-start | bytes 393220
  124.6 18.0 %copy-start.7 = (f32[4,8,32,128]{3,1,2,0:T(8,128)S(1)}, f32[4,8,32,128]{3,1,2,0:T(8,128)}, u32[]{:S(2)}) copy-start(f32[4,8,32,128]{3,1,2,0:T(8,128)} %fusion.98) | copy-start | bytes 1572868
  124.6 18.0 %copy-start.15 = (f32[8,32,128]{2,0,1:T(8,128)S(1)}, f32[8,32,128]{2,0,1:T(8,128)}, u32[]{:S(2)}) copy-start(f32[8,32,128]{2,0,1:T(8,128)} %copy-done.14) | copy-start | bytes 393220
  124.6 18.0 %copy-start.17 = (f32[8,32,128]{2,1,0:T(8,128)S(1)}, f32[8,32,128]{2,1,0:T(8,128)}, u32[]{:S(2)}) copy-start(f32[8,32,128]{2,1,0:T(8,128)} %param.8) | copy-start | bytes 393220
  128.1 14.8 %copy-start.24 = (f32[128,128,1,1]{1,0,3,2:T(8,128)S(1)}, f32[128,128,1,1]{1,0,3,2:T(8,128)}, u32[]{:S(2)}) copy-start(f32[128,128,1,1]{1,0,3,2:T(8,128)} %constant.34) | copy-start | bytes 196612
  128.1 24.8 %all-to-all-start.3 = ((f32[16,1,10240]{2,1,0:T(1,128)}), f32[16,1,10240]{2,1,0:T(1,128)S(1)}, u32[]{:S(2)}, u32[]{:S(2)}) async-start(f32[16,1,10240]{2,1,0:T(1,128)} %reshape.38), calls=%async_computation.3 | async-start | bytes 1310720 | tf_op jit(solution)/shard_map/all_to_all | solution.py:149
  134.9 27.6 %collective-permute-start.2 = (f32[5,4,32,128]{3,1,2,0:T(4,128)}, f32[5,4,32,128]{3,1,2,0:T(4,128)}, u32[]{:S(2)}, u32[]{:S(2)}) collective-permute-start(f32[5,4,32,128]{3,1,2,0:T(4,128)} %get-tuple-element.24), channel_id=1, source_target_pairs={{0,16},{16,32},{32,48},{48,64},{64,80},{80,96},{96,112},{112,128},... | collective-permute-start | bytes 983048 | tf_op jit(solution)/shard_map/ppermute | solution.py:28
  136.8 25.7 %collective-permute-start.3 = (f32[5,4,32,128]{3,1,2,0:T(4,128)}, f32[5,4,32,128]{3,1,2,0:T(4,128)}, u32[]{:S(2)}, u32[]{:S(2)}) collective-permute-start(f32[5,4,32,128]{3,1,2,0:T(4,128)} %get-tuple-element.25), channel_id=1, source_target_pairs={{16,0},{32,16},{48,32},{64,48},{80,64},{96,80},{112,96},{128,112},... | collective-permute-start | bytes 983048 | tf_op jit(solution)/shard_map/ppermute | solution.py:29
  159.8 2.7 %copy-start.10 = (f32[5,8,32,128]{3,1,2,0:T(8,128)S(1)}, f32[5,8,32,128]{3,1,2,0:T(8,128)}, u32[]{:S(2)}) copy-start(f32[5,8,32,128]{3,1,2,0:T(8,128)} %copy-done.8) | copy-start | bytes 1966084
  159.8 2.7 %copy-start.11 = (f32[5,8,32,128]{3,1,2,0:T(8,128)S(1)}, f32[5,8,32,128]{3,1,2,0:T(8,128)}, u32[]{:S(2)}) copy-start(f32[5,8,32,128]{3,1,2,0:T(8,128)} %fusion.103) | copy-start | bytes 1966084
  159.8 2.7 %copy-start.21 = (f32[1,8,32,128]{3,1,2,0:T(8,128)S(1)}, f32[1,8,32,128]{3,1,2,0:T(8,128)}, u32[]{:S(2)}) copy-start(f32[1,8,32,128]{3,1,2,0:T(8,128)} %get-tuple-element.33) | copy-start | bytes 393220
  159.8 2.7 %copy-start.22 = (f32[1,8,32,128]{3,1,2,0:T(8,128)S(1)}, f32[1,8,32,128]{3,1,2,0:T(8,128)}, u32[]{:S(2)}) copy-start(f32[1,8,32,128]{3,1,2,0:T(8,128)} %get-tuple-element.34) | copy-start | bytes 393220
  (2 other events, 1.7 us)
